TPU v7x, 128 devices: a whole 4x4x4 slice. The times are simulated.
128 devices in a mesh: dp: 16 (over x, z_hi, core), tm: 8 (over z_lo, y).
Axes of the slice: x: 4, y: 4, z: 4 (z_hi: 2, z_lo: 2; z = z_hi * 2 + z_lo), core: 2. Of those that a mesh axis runs over, the one named last changes fastest.
Arguments:
- loaded: bfloat16 [16, 64, 16, 16, 256], P('dp', 'tm')
- lengths: int32 [16, 8], P('dp'), may hold values from 1 to 8, as said below
- resolution: int32 [16, 2], P('dp'), may hold values from 8 to 16, as said below
- weight: bfloat16 [27, 256, 256], replicated, may hold values from -0.078125 to 0.078125
- norm_gain: float32 [256], replicated, may hold values from 0.1 to 1.9
- norm_bias: float32 [256], replicated, may hold values from -3 to 3
- cotangent: bfloat16 [16, 64, 16, 16, 256], P('dp', 'tm'), may hold values from -6 to 6
Outputs:
- encoded: bfloat16 [16, 64, 16, 16, 256], P('dp', 'tm')
- input_grad: bfloat16 [16, 64, 16, 16, 256], P('dp', 'tm')
- weight_grad: float32 [27, 256, 256], replicated
- gain_grad: float32 [256], replicated
- bias_grad: float32 [256], replicated
Inputs may be any that keep to these rules, and one draw needn't show every extreme that they name: `lengths`: row c lists how many consecutive frames of clip c each index of tm loaded, in frame order; the row sums to the clip's frame count, which is 64 - k for some 0 <= k <= 8, so that every loaded frame belongs to the loader's own temporal slab or to the one before it; in every draw one clip has all 64 frames, 8 on every index. `resolution`: valid rows (column 0) and columns (column 1) of clip c; frames are padded at the bottom and right; at least 8 rows and 8 columns, and in every draw one clip has the full 16 by 16.
All inputs are finite; a program needn't handle non-finite values.
Results may differ from a plain program's by a relative error of at most 0.0046.
The roundings to bfloat16 on the way count: a program that leaves them out, or rounds other values in their place, can miss the bound.
Values may be sent and summed in bfloat16 or wider, within the bound.
A program may use at most 128 MiB of HBM per device.

v0:
```python
import math
import jax
import jax.numpy as jnp
from jax import lax
from jax.sharding import PartitionSpec as P

GROUPS = 32
EPSILON = 1e-05


def shifted(block, axis, distance):
    devices = range(lax.axis_size(axis))
    route = [(i - distance, i) for i in devices if i - distance in devices]
    return lax.ppermute(block, axis, route)


def group_total(values):
    shaped = values.reshape(values.shape[:-1] + (GROUPS, values.shape[-1] // GROUPS))
    return jnp.sum(shaped, axis=(0, 1, 2, 4))


def spread_groups(per_group, channels):
    return jnp.repeat(per_group, channels // per_group.shape[0])


def tap_sweeps(past_pad, future_pad, weight, frames, frame_rows, frame_cols):
    channels = weight.shape[2]
    positions = frames * frame_rows * frame_cols
    forward = jnp.zeros((positions, channels), jnp.float32)
    backward = jnp.zeros((positions, channels), jnp.float32)
    grad_flat = future_pad[:frames, 1 : frame_rows + 1, 1 : frame_cols + 1].reshape(
        positions, channels
    )
    kernel_parts = []
    for time_tap in range(3):
        for row_tap in range(3):
            for col_tap in range(3):
                tap_index = time_tap * 9 + row_tap * 3 + col_tap
                past_slice = past_pad[
                    time_tap : time_tap + frames,
                    row_tap : row_tap + frame_rows,
                    col_tap : col_tap + frame_cols,
                ].reshape(positions, channels)
                forward = forward + jnp.dot(
                    past_slice, weight[tap_index], preferred_element_type=jnp.float32
                )
                kernel_parts.append(
                    lax.dot_general(
                        past_slice,
                        grad_flat,
                        (((0,), (0,)), ((), ())),
                        preferred_element_type=jnp.float32,
                    )
                )
                future_slice = future_pad[
                    2 - time_tap : 2 - time_tap + frames,
                    2 - row_tap : 2 - row_tap + frame_rows,
                    2 - col_tap : 2 - col_tap + frame_cols,
                ].reshape(positions, channels)
                backward = backward + lax.dot_general(
                    future_slice,
                    weight[tap_index],
                    (((1,), (1,)), ((), ())),
                    preferred_element_type=jnp.float32,
                )
    return (forward, backward, jnp.stack(kernel_parts))


def place_frames(own_frames, slab_start, first_frame, own_length):
    frames = own_frames.shape[0]
    offset = slab_start + jnp.arange(frames, dtype=jnp.int32) - first_frame
    usable = (offset >= 0) & (offset < own_length)
    picked = jnp.take(own_frames, jnp.clip(offset, 0, frames - 1), axis=0)
    return picked * usable.astype(jnp.bfloat16)[:, None, None, None]


def body(loaded, lengths, resolution, weight, norm_gain, norm_bias, cotangent):
    own_frames = loaded[0]
    frames, frame_rows, frame_cols, channels = own_frames.shape
    slab_count = lax.axis_size("tm")
    own_slab = lax.axis_index("tm")
    length_row = lengths[0]
    starts = jnp.cumsum(length_row) - length_row
    frame_total = jnp.sum(length_row)
    first_frame = starts[own_slab]
    own_length = length_row[own_slab]
    staying = place_frames(own_frames, own_slab * frames, first_frame, own_length)
    leaving = place_frames(own_frames, (own_slab - 1) * frames, first_frame, own_length)
    arrived = shifted(leaving, "tm", -1)
    assembled = staying.astype(jnp.float32) + arrived.astype(jnp.float32)
    frame_ids = own_slab * frames + jnp.arange(frames, dtype=jnp.int32)
    live_rows = jnp.arange(frame_rows, dtype=jnp.int32) < resolution[0, 0]
    live_cols = jnp.arange(frame_cols, dtype=jnp.int32) < resolution[0, 1]
    live_cells = (
        (frame_ids < frame_total)[:, None, None]
        & live_rows[None, :, None]
        & live_cols[None, None, :]
    ).astype(jnp.float32)[..., None]
    inputs_f = assembled * live_cells
    cell_count = (frame_total * resolution[0, 0] * resolution[0, 1] * (channels // GROUPS)).astype(
        jnp.float32
    )
    group_means = lax.psum(group_total(inputs_f), "tm") / cell_count
    centred = (inputs_f - spread_groups(group_means, channels)) * live_cells
    variance = lax.psum(group_total(centred * centred), "tm") / cell_count
    inverse_root = spread_groups(lax.rsqrt(variance + EPSILON), channels)
    normed = centred * inverse_root
    pre_activation = normed * norm_gain + norm_bias
    gate_value = jax.nn.sigmoid(pre_activation)
    activation = (pre_activation * gate_value * live_cells).astype(jnp.bfloat16)
    earlier = shifted(activation[frames - 2 :], "tm", 1)
    past_pad = jnp.pad(
        jnp.concatenate([earlier, activation], axis=0), ((0, 0), (1, 1), (1, 1), (0, 0))
    )
    masked_grad = cotangent[0] * live_cells.astype(jnp.bfloat16)
    future = shifted(masked_grad[:2], "tm", -1)
    future_pad = jnp.pad(
        jnp.concatenate([masked_grad, future], axis=0), ((0, 0), (1, 1), (1, 1), (0, 0))
    )
    forward, backward, kernel_part = tap_sweeps(
        past_pad, future_pad, weight, frames, frame_rows, frame_cols
    )
    encoded = (forward.reshape(frames, frame_rows, frame_cols, channels) * live_cells).astype(
        jnp.bfloat16
    )
    activation_grad = backward.reshape(frames, frame_rows, frame_cols, channels) * live_cells
    pre_grad = activation_grad * gate_value * (1.0 + pre_activation * (1.0 - gate_value))
    gain_part = jnp.sum(pre_grad * normed, axis=(0, 1, 2))
    bias_part = jnp.sum(pre_grad, axis=(0, 1, 2))
    normed_grad = pre_grad * norm_gain
    normed_sum, projected_sum = lax.psum(
        (group_total(normed_grad), group_total(normed_grad * normed)), "tm"
    )
    grad_mean = spread_groups(normed_sum / cell_count, channels)
    grad_proj = spread_groups(projected_sum / cell_count, channels)
    input_grad = (
        inverse_root * (normed_grad - grad_mean - normed * grad_proj) * live_cells
    ).astype(jnp.bfloat16)
    kernel_sum, gain_sum, bias_sum = lax.psum((kernel_part, gain_part, bias_part), ("dp", "tm"))
    grad_scale = 1.0 / math.sqrt(
        lax.axis_size("dp") * slab_count * frames * frame_rows * frame_cols
    )
    return (
        encoded[None],
        input_grad[None],
        kernel_sum * grad_scale,
        gain_sum * grad_scale,
        bias_sum * grad_scale,
    )


def solution(mesh):
    placed = (
        P("dp", "tm", None, None, None),
        P("dp", None),
        P("dp", None),
        P(),
        P(),
        P(),
        P("dp", "tm", None, None, None),
    )
    return jax.shard_map(
        body,
        mesh=mesh,
        in_specs=placed,
        out_specs=(P("dp", "tm", None, None, None), P("dp", "tm", None, None, None), P(), P(), P()),
        check_vma=False,
    )
```

profile of v0, /device:TPU:1, one launch (start us, length us, event | category | flops | bytes accessed | tf_op | source)
XLA Modules:
  0.0 453.0 jit_solution(18382396377118999737)
XLA Ops:
  8.8 1.2 constant_dynamic-slice_fusion
  10.6 1.3 compare_and_fusion
  13.7 1.3 collective-permute-start
  19.5 1.3 collective-permute-start.2
  20.8 1.3 compare_and_fusion.1
  24.6 2.5 broadcast_multiply_fusion.1
  27.2 18.9 %collective-permute-done.2 = bf16[2,16,16,256]{3,2,1,0:T(8,128)(2,1)S(1)} collective-permute-done((bf16[2,16,16,256]{3,2,1,0:T(8,128)(2,1)}, bf16[2,16,16,256]{3,2,1,0:T(8,128)(2,1)S(1)}, u32[]{:S(2)}, u32[]{:S(2)}) %collective-permute-start.2) | collective-permute-done | bytes 262176 | tf_op jit(solution)/shard_map/ppermute | solution.py:14
  46.2 7.1 %pad_slice_fusion = (bf16[8,16,16,256]{3,2,1,0:T(8,128)(2,1)}, bf16[8,16,16,256]{3,2,1,0:T(8,128)(2,1)}, bf16[8,16,16,256]{3,2,1,0:T(8,128)(2,1)}, bf16[8,16,16,...) fusion(bf16[10,16,16,256]{3,2,1,0:T(8,128)(2,1)S(1)} %pad_maxim, ...), kind=kLoop, calls=%fused_computation.2 | loop fusion | bytes 21233664 | tf_op jit(solution)/shard_map/slice | solution.py:55
  53.3 2.4 pad_slice_fusion.1
  82.5 1.8 convolution_add_fusion
  84.3 1.8 fusion
  86.3 15.2 %psum.49 = f32[32]{0:T(128)S(1)} all-reduce(f32[32]{0:T(128)S(1)} %reduce_sum.76), channel_id=1, replica_groups=mesh['dp'=16,'tm'=8] {'tm'}, use_global_device_ids=true, to_apply=%region_4.6 | all-reduce | flops 32 | bytes 256 | tf_op jit(solution)/shard_map/psum | solution.py:103
  101.7 2.0 multiply_reduce_fusion.2
  103.9 25.4 %psum.50 = f32[32]{0:T(128)S(1)} all-reduce(f32[32]{0:T(128)S(1)} %reduce_sum.97), channel_id=1, replica_groups=mesh['dp'=16,'tm'=8] {'tm'}, use_global_device_ids=true, to_apply=%region_7.9 | all-reduce | flops 32 | bytes 256 | tf_op jit(solution)/shard_map/psum | solution.py:105
  129.4 4.7 %multiply_reduce_fusion = (f32[256]{0:T(256)S(1)}, f32[256]{0:T(256)S(1)}, f32[256]{0:T(256)S(1)}, f32[256]{0:T(256)S(1)}, f32[8,16,16,256]{3,2,1,0:T(8,128)}, /*index=5*/bf16[8,16,16,256]{3,2,1,0:T(8,128)(2,1)S(1)}) fusion(f32[256]{0:T(256)S(1)} %mul.181, f32[256]{0:T(256)S(1)} %sub.55, f32[8,16,16]{2,1,0:T(8,128)S(1)} %get-tuple-element.73, ...), kind=kLoop, calls=%fused_computation.103 | loop fusion | flops 15727616 | bytes 7356440 | tf_op jit(solution)/shard_map/reduce_sum | solution.py:128
  134.9 2.9 collective-permute-start.1
  138.2 15.0 %all-reduce.3 = (f32[32]{0:T(128)S(1)}, f32[32]{0:T(128)S(1)}) all-reduce(f32[32]{0:T(128)S(1)} %reduce_sum.103, f32[32]{0:T(128)S(1)} %reduce_sum.100), channel_id=1, replica_groups=mesh['dp'=16,'tm'=8] {'tm'}, use_global_device_ids=true, to_apply=%region_13.15 | all-reduce | flops 64 | bytes 512 | tf_op jit(solution)/shard_map/psum | solution.py:131
  153.6 80.1 %all-reduce.2 = (f32[256]{0:T(256)S(1)}, f32[256]{0:T(256)S(1)}) all-reduce(f32[256]{0:T(256)S(1)} %get-tuple-element.6, f32[256]{0:T(256)S(1)} %get-tuple-element.9), channel_id=1, replica_groups=mesh['dp'=16,'tm'=8] {'dp','tm'}, use_global_device_ids=true, to_apply=%region_16.18 | all-reduce | flops 512 | bytes 4096 | tf_op jit(solution)/shard_map/psum | solution.py:139
  233.6 3.9 fusion.33
  238.8 7.0 %pad_slice_fusion.24 = (bf16[8,16,16,256]{3,2,1,0:T(8,128)(2,1)}, bf16[8,16,16,256]{3,2,1,0:T(8,128)(2,1)S(1)}, bf16[8,16,16,256]{3,2,1,0:T(8,128)(2,1)}, bf16[8...) fusion(bf16[10,16,16,256]{3,2,1,0:T(8,128)(2,1)S(1)} %pad_maxim, ...), kind=kLoop, calls=%fused_computation.26 | loop fusion | bytes 21233664 | tf_op jit(solution)/shard_map/slice | solution.py:39
  245.8 2.7 pad_slice_fusion.25
  249.7 2.7 fusion.86
  252.4 1.2 fusion.27
  253.6 1.2 fusion.26
  254.8 1.2 fusion.25
  257.2 1.2 fusion.24
  258.4 1.2 fusion.23
  259.6 1.2 fusion.22
  260.8 1.2 fusion.21
  263.2 1.2 fusion.19
  264.4 1.2 fusion.18
  265.6 1.2 fusion.17
  267.9 1.2 fusion.16
  269.1 1.2 fusion.15
  270.3 1.2 fusion.14
  271.6 1.2 fusion.13
  273.9 1.2 fusion.11
  275.1 1.2 fusion.10
  276.3 1.2 fusion.9
  278.7 1.2 fusion.7
  279.9 1.2 fusion.6
  281.1 1.2 fusion.5
  282.3 1.2 fusion.4
  283.5 1.2 copy-done.8
  284.8 2.2 convolution_add_fusion.51
  315.6 1.3 multiply_convert_fusion.1
  316.9 122.3 %all-reduce.6.cloned.1.call-done = f32[27,256,256]{2,1,0:T(8,128)} async-done(((f32[27,256,256]{2,1,0:T(8,128)}), f32[27,256,256]{2,1,0:T(8,128)}) %all-reduce.6.cloned.1.call-update) | async-done | bytes 7077904 | tf_op jit(solution)/shard_map/psum | solution.py:139
  439.2 6.8 %broadcast_multiply_fusion = f32[27,256,256]{2,1,0:T(8,128)} fusion(f32[27,256,256]{2,1,0:T(8,128)} %all-reduce.6.cloned.1.call-done), kind=kLoop, calls=%fused_computation.50 | loop fusion | flops 1769472 | bytes 14155776 | tf_op jit(solution)/shard_map/mul | solution.py:146
  (206 shorter events, 74.6 us)
Async XLA Ops:
  7.2 4.8 %copy-start = (bf16[1,8,16,16,256]{4,3,2,1,0:T(8,128)(2,1)S(1)}, bf16[1,8,16,16,256]{4,3,2,1,0:T(8,128)(2,1)}, u32[]{:S(2)}) copy-start(bf16[1,8,16,16,256]{4,3,2,1,0:T(8,128)(2,1)} %param.9) | copy-start | bytes 3145732
  7.2 432.0 %all-reduce.6.cloned.1.call-start = ((), (), s32[]{:S(2)}) async-start(), calls=%async_computation | async-start | bytes 14155776 | tf_op jit(solution)/shard_map/psum | solution.py:139
  11.9 3.1 copy-start.50
  12.0 3.7 copy-start.48
  12.0 6.5 %copy-start.4 = (bf16[1,8,16,16,256]{4,3,2,1,0:T(8,128)(2,1)S(1)}, bf16[1,8,16,16,256]{4,3,2,1,0:T(8,128)(2,1)}, u32[]{:S(2)}) copy-start(bf16[1,8,16,16,256]{4,3,2,1,0:T(8,128)(2,1)} %param.15) | copy-start | bytes 3145732
  13.7 70.5 %collective-permute-start = (bf16[8,16,16,256]{3,2,1,0:T(8,128)(2,1)}, bf16[8,16,16,256]{3,2,1,0:T(8,128)(2,1)}, u32[]{:S(2)}, u32[]{:S(2)}) collective-permute-start(bf16[8,16,16,256]{3,2,1,0:T(8,128)(2,1)} %select_multiply_fusion), channel_id=1, source_target_pairs={{1,0},{2,1},{3,2},{4,3},{5,4},{6,5},{7,6},{9,8},{10,9},{11,10},{12... | collective-permute-start | bytes 3145736 | tf_op jit(solution)/shard_map/ppermute | solution.py:14
  19.5 26.6 %collective-permute-start.2 = (bf16[2,16,16,256]{3,2,1,0:T(8,128)(2,1)}, bf16[2,16,16,256]{3,2,1,0:T(8,128)(2,1)S(1)}, u32[]{:S(2)}, u32[]{:S(2)}) collective-permute-start(bf16[2,16,16,256]{3,2,1,0:T(8,128)(2,1)} %slice.379), channel_id=1, source_target_pairs={{1,0},{2,1},{3,2},{4,3},{5,4},{6,5},{7,6},{9,8},{10,9},{11,10},{12... | collective-permute-start | bytes 786440 | tf_op jit(solution)/shard_map/ppermute | solution.py:14
  53.3 2.4 copy-start.2
  53.3 2.4 copy-start.10
  56.2 1.2 copy-start.46
  57.4 1.2 copy-start.45
  59.3 1.2 copy-start.44
  61.7 1.2 copy-start.42
  62.9 1.2 copy-start.41
  64.2 1.2 copy-start.40
  65.4 1.2 copy-start.39
  66.6 1.2 copy-start.38
  69.5 1.2 copy-start.36
  70.8 1.2 copy-start.35
  72.0 1.2 copy-start.34
  74.4 1.2 copy-start.32
  75.7 1.2 copy-start.31
  76.9 1.2 copy-start.30
  78.6 1.2 copy-start.9
  81.3 1.2 copy-start.29
  84.3 45.1 %copy-start.47 = (f32[256]{0:T(256)S(1)}, f32[256]{0:T(256)}, u32[]{:S(2)}) copy-start(f32[256]{0:T(256)} %param.13) | copy-start | bytes 3076
  84.3 45.1 %copy-start.49 = (f32[256]{0:T(256)S(1)}, f32[256]{0:T(256)}, u32[]{:S(2)}) copy-start(f32[256]{0:T(256)} %param.14) | copy-start | bytes 3076
  134.9 103.9 %collective-permute-start.1 = (bf16[2,16,16,256]{3,2,1,0:T(8,128)(2,1)}, bf16[2,16,16,256]{3,2,1,0:T(8,128)(2,1)S(1)}, u32[]{:S(2)}, u32[]{:S(2)}) collective-permute-start(bf16[2,16,16,256]{3,2,1,0:T(8,128)(2,1)} %slice.374), channel_id=1, source_target_pairs={{0,1},{1,2},{2,3},{3,4},{4,5},{5,6},{6,7},{8,9},{9,10},{10,11},{11... | collective-permute-start | bytes 786440 | tf_op jit(solution)/shard_map/ppermute | solution.py:14
  284.7 2.7 copy-start.3
  284.7 3.0 copy-start.28
  287.7 1.5 copy-start.27
  290.1 1.2 copy-start.26
  291.3 1.2 copy-start.25
  292.5 1.3 copy-start.24
  293.8 1.3 copy-start.23
  295.0 1.2 copy-start.22
  297.5 1.3 copy-start.20
  298.8 1.3 copy-start.19
  300.5 1.3 copy-start.18
  301.7 1.3 copy-start.17
  303.0 1.2 copy-start.16
  305.4 1.3 copy-start.14
  306.7 1.3 copy-start.13
  309.2 1.3 copy-start.7
  310.9 1.3 copy-start.6
  312.2 1.3 copy-start.5
  313.9 1.3 copy-start.11
  439.2 6.8 %copy-start.1 = (bf16[1,8,16,16,256]{4,3,2,1,0:T(8,128)(2,1)S(1)}, bf16[1,8,16,16,256]{4,3,2,1,0:T(8,128)(2,1)}, u32[]{:S(2)}) copy-start(bf16[1,8,16,16,256]{4,3,2,1,0:T(8,128)(2,1)} %param.9) | copy-start | bytes 3145732
  (7 other events, 8.6 us)
Sparse Core Ops, SparseCore 0:
  283.7 155.4 all-reduce.5
where the time goes:
time: 458 us; the launch traced here: 453 us
  waiting for transfers between devices  141 us (31%)
  blocking collectives  136 us (30%)
  matrix products  62.2 us (14%)
  local copies, waits for them, and re-layouts  58 us (13%)
  other arithmetic  33.6 us (7%)
  between operations  16.9 us (4%)
  starting transfers between devices  5.49 us (1%)
    psum x1, waiting for transfers between devices, body(): lax.psum((kernel_part, gain_part, bias_part), ('dp', 'tm'))  122 us
    psum x1, blocking collectives, body(): lax.psum((kernel_part, gain_part, bias_part), ('dp', 'tm'))  80.1 us
    unnamed x102, local copies, waits for them, and re-layouts  32.7 us
    dot_general x27, matrix products, tap_sweeps(): lax.dot_general(past_slice, grad_flat, (((0,), (0,)), ((), ())), preferre...  32.2 us
    psum x1, blocking collectives, body(): variance = lax.psum(group_total(centred * centred), 'tm') / cell_count  25.4 us
    ppermute x3, waiting for transfers between devices, shifted(): return lax.ppermute(block, axis, route)  18.9 us
    dot_general x27, matrix products, tap_sweeps(): jnp.dot(past_slice, weight[tap_index], preferred_element_type=jnp.float32)  16 us
    psum x1, blocking collectives, body(): group_means = lax.psum(group_total(inputs_f), 'tm') / cell_count  15.2 us
  transfers between devices with their start and end apart: 4, of which 2 were waited for; matrix products, arithmetic and copies ran while one was open for 12% of the time, Pallas kernels for 0%

commit v1 on v0

--- a/solution.py
+++ b/solution.py
@@ -136,7 +136,9 @@
     input_grad = (
         inverse_root * (normed_grad - grad_mean - normed * grad_proj) * live_cells
     ).astype(jnp.bfloat16)
-    kernel_sum, gain_sum, bias_sum = lax.psum((kernel_part, gain_part, bias_part), ("dp", "tm"))
+    kernel_sum, gain_sum, bias_sum = lax.psum(
+        lax.psum((kernel_part, gain_part, bias_part), "tm"), "dp"
+    )
     grad_scale = 1.0 / math.sqrt(
         lax.axis_size("dp") * slab_count * frames * frame_rows * frame_cols
     )

time: 458 us -> 535 us (1.17)
  waiting for transfers between devices: 141 us -> 218 us
  local copies, waits for them, and re-layouts: 58 us -> 51.7 us
    psum x1 -> x2, waiting for transfers between devices: 122 us -> 195 us  [the longest x1 158 us: body(): lax.psum(lax.psum((kernel_part, gain_part, bias_part), 'tm'), 'dp')]
    psum x1, blocking collectives: 25.4 us -> 12.5 us  [body(): variance = lax.psum(group_total(centred * centred), 'tm') / cell_count]
    psum x1, blocking collectives: 80.1 us -> 92 us  [body(): lax.psum(lax.psum((kernel_part, gain_part, bias_part), 'tm'), 'dp')]
    unnamed x102 -> x108, local copies, waits for them, and re-layouts: 32.7 us -> 27.1 us
  transfers between devices with their start and end apart: 4 -> 5, of which waited for: 2 -> 4; matrix products, arithmetic and copies ran while one was open for 12% -> 13% of each run, Pallas kernels for 0% -> 0%
where the time goes in v1:
time: 535 us; the launch traced here: 529 us
  waiting for transfers between devices  218 us (41%)
  blocking collectives  136 us (25%)
  matrix products  66.7 us (12%)
  local copies, waits for them, and re-layouts  51.7 us (10%)
  other arithmetic  33.8 us (6%)
  between operations  17 us (3%)
  starting transfers between devices  6.14 us (1%)
    psum x1, waiting for transfers between devices, body(): lax.psum(lax.psum((kernel_part, gain_part, bias_part), 'tm'), 'dp')  158 us
    psum x1, blocking collectives, body(): lax.psum(lax.psum((kernel_part, gain_part, bias_part), 'tm'), 'dp')  92 us
    psum x1, waiting for transfers between devices, body(): lax.psum((kernel_part, gain_part, bias_part), 'tm')  37.5 us
    dot_general x27, matrix products, tap_sweeps(): lax.dot_general(past_slice, grad_flat, (((0,), (0,)), ((), ())), preferre...  32 us
    unnamed x108, local copies, waits for them, and re-layouts  27.1 us
    ppermute x3, waiting for transfers between devices, shifted(): return lax.ppermute(block, axis, route)  22.9 us
    dot_general x27, matrix products, tap_sweeps(): jnp.dot(past_slice, weight[tap_index], preferred_element_type=jnp.float32)  20.8 us
    psum x1, blocking collectives, body(): lax.psum((group_total(normed_grad), group_total(normed_grad * normed)), '...  16.2 us
  transfers between devices with their start and end apart: 5, of which 4 were waited for; matrix products, arithmetic and copies ran while one was open for 13% of the time, Pallas kernels for 0%

profile of v1, /device:TPU:1, one launch (start us, length us, event | category | flops | bytes accessed | tf_op | source)
XLA Modules:
  0.0 529.4 jit_solution(5921603355026780784)
XLA Ops:
  8.8 1.2 constant_dynamic-slice_fusion
  10.6 1.3 compare_and_fusion
  13.7 1.3 collective-permute-start
  19.5 1.3 collective-permute-start.2
  20.8 1.3 compare_and_fusion.1
  24.7 1.6 broadcast_multiply_fusion.1
  26.2 19.8 %collective-permute-done.2 = bf16[2,16,16,256]{3,2,1,0:T(8,128)(2,1)S(1)} collective-permute-done((bf16[2,16,16,256]{3,2,1,0:T(8,128)(2,1)}, bf16[2,16,16,256]{3,2,1,0:T(8,128)(2,1)S(1)}, u32[]{:S(2)}, u32[]{:S(2)}) %collective-permute-start.2) | collective-permute-done | bytes 262176 | tf_op jit(solution)/shard_map/ppermute | solution.py:14
  46.2 7.1 %pad_slice_fusion = (bf16[8,16,16,256]{3,2,1,0:T(8,128)(2,1)}, bf16[8,16,16,256]{3,2,1,0:T(8,128)(2,1)}, bf16[8,16,16,256]{3,2,1,0:T(8,128)(2,1)}, bf16[8,16,16,...) fusion(bf16[10,16,16,256]{3,2,1,0:T(8,128)(2,1)S(1)} %pad_maxim, ...), kind=kLoop, calls=%fused_computation.2 | loop fusion | bytes 21233664 | tf_op jit(solution)/shard_map/slice | solution.py:55
  53.3 2.5 pad_slice_fusion.1
  81.8 1.8 convolution_add_fusion
  83.6 1.8 fusion
  85.6 15.2 %psum.70 = f32[32]{0:T(128)S(1)} all-reduce(f32[32]{0:T(128)S(1)} %reduce_sum.76), channel_id=1, replica_groups=mesh['dp'=16,'tm'=8] {'tm'}, use_global_device_ids=true, to_apply=%region_4.6 | all-reduce | flops 32 | bytes 256 | tf_op jit(solution)/shard_map/psum | solution.py:103
  101.0 2.0 multiply_reduce_fusion.2
  103.2 12.5 %psum.71 = f32[32]{0:T(128)S(1)} all-reduce(f32[32]{0:T(128)S(1)} %reduce_sum.97), channel_id=1, replica_groups=mesh['dp'=16,'tm'=8] {'tm'}, use_global_device_ids=true, to_apply=%region_7.9 | all-reduce | flops 32 | bytes 256 | tf_op jit(solution)/shard_map/psum | solution.py:105
  115.9 4.8 multiply_reduce_fusion
  120.7 3.5 collective-permute-start.1
  124.2 3.1 collective-permute-done.1
  133.4 1.2 fusion.24
  134.6 1.2 fusion.23
  135.7 1.2 fusion.22
  136.9 1.2 fusion.21
  141.7 1.2 fusion.17
  144.0 1.2 fusion.16
  145.2 1.2 fusion.15
  146.4 1.2 fusion.14
  147.6 1.2 fusion.13
  152.3 1.2 fusion.9
  155.9 1.2 fusion.6
  157.1 1.2 fusion.5
  158.3 1.2 fusion.4
  159.9 16.2 %all-reduce.3 = (f32[32]{0:T(128)S(1)}, f32[32]{0:T(128)S(1)}, f32[256]{0:T(256)S(1)}, f32[256]{0:T(256)S(1)}) all-reduce(f32[32]{0:T(128)S(1)} %reduce_sum.103, f32[32]{0:T(128)S(1)} %reduce_sum.100, f32[256]{0:T(256)S(1)} %get-tuple-element.6, f32[256]{0:T(256)S(1)} %get-tuple-element.9), channel_id=1, replica_groups=mesh['dp'=16,'tm'=8] {'tm'}, use_global_device_ids=true, to_apply=%region_13.15 | all-reduce | flops 576 | bytes 4608 | tf_op jit(solution)/shard_map/psum | solution.py:131
  176.5 92.0 %all-reduce.2 = (f32[256]{0:T(256)S(1)}, f32[256]{0:T(256)S(1)}) all-reduce(f32[256]{0:T(256)S(1)} %get-tuple-element.14, f32[256]{0:T(256)S(1)} %get-tuple-element.15), channel_id=1, replica_groups=mesh['dp'=16,'tm'=8] {'dp'}, use_global_device_ids=true, to_apply=%region_18.20 | all-reduce | flops 512 | bytes 4096 | tf_op jit(solution)/shard_map/psum | solution.py:139
  269.6 4.0 fusion.33
  274.7 2.8 pad_slice_fusion.25
  277.5 6.9 %pad_slice_fusion.24 = (bf16[8,16,16,256]{3,2,1,0:T(8,128)(2,1)}, bf16[8,16,16,256]{3,2,1,0:T(8,128)(2,1)S(1)}, bf16[8,16,16,256]{3,2,1,0:T(8,128)(2,1)}, bf16[8...) fusion(bf16[10,16,16,256]{3,2,1,0:T(8,128)(2,1)S(1)} %pad_maxim, ...), kind=kLoop, calls=%fused_computation.26 | loop fusion | bytes 21233664 | tf_op jit(solution)/shard_map/slice | solution.py:39
  284.5 1.3 fusion.86
  285.8 1.5 convolution_add_fusion.51
  287.3 1.4 convolution_add_fusion.50
  288.7 1.3 convolution_add_fusion.49
  290.1 1.4 convolution_add_fusion.48
  291.6 1.4 convolution_add_fusion.47
  293.0 1.4 convolution_add_fusion.46
  294.5 1.3 convolution_add_fusion.45
  295.8 37.5 %all-reduce.7.cloned.1.call-done = f32[27,256,256]{2,1,0:T(8,128)} async-done(((f32[27,256,256]{2,1,0:T(8,128)}), f32[27,256,256]{2,1,0:T(8,128)}) %all-reduce.7.cloned.1.call-update) | async-done | bytes 7077904 | tf_op jit(solution)/shard_map/psum | solution.py:140
  333.3 1.8 convolution_add_fusion.44
  356.5 1.3 multiply_convert_fusion.1
  357.8 157.7 %all-reduce.9.cloned.1.call-done = f32[27,256,256]{2,1,0:T(8,128)} async-done(((f32[27,256,256]{2,1,0:T(8,128)}), f32[27,256,256]{2,1,0:T(8,128)}) %all-reduce.9.cloned.1.call-update) | async-done | bytes 7077904 | tf_op jit(solution)/shard_map/psum | solution.py:139
  515.6 6.8 %broadcast_multiply_fusion = f32[27,256,256]{2,1,0:T(8,128)} fusion(f32[27,256,256]{2,1,0:T(8,128)} %all-reduce.9.cloned.1.call-done), kind=kLoop, calls=%fused_computation.50 | loop fusion | flops 1769472 | bytes 14155776 | tf_op jit(solution)/shard_map/mul | solution.py:148
  (215 shorter events, 76.7 us)
Async XLA Ops:
  7.2 4.8 copy-start
  7.2 326.1 %all-reduce.7.cloned.1.call-start = ((), (), s32[]{:S(2)}) async-start(), calls=%async_computation | async-start | bytes 14155776 | tf_op jit(solution)/shard_map/psum | solution.py:140
  11.9 3.1 copy-start.53
  12.0 3.8 copy-start.51
  12.0 6.5 %copy-start.6 = (bf16[1,8,16,16,256]{4,3,2,1,0:T(8,128)(2,1)S(1)}, bf16[1,8,16,16,256]{4,3,2,1,0:T(8,128)(2,1)}, u32[]{:S(2)}) copy-start(bf16[1,8,16,16,256]{4,3,2,1,0:T(8,128)(2,1)} %param.15) | copy-start | bytes 3145732
  13.7 69.9 %collective-permute-start = (bf16[8,16,16,256]{3,2,1,0:T(8,128)(2,1)}, bf16[8,16,16,256]{3,2,1,0:T(8,128)(2,1)}, u32[]{:S(2)}, u32[]{:S(2)}) collective-permute-start(bf16[8,16,16,256]{3,2,1,0:T(8,128)(2,1)} %select_multiply_fusion), channel_id=1, source_target_pairs={{1,0},{2,1},{3,2},{4,3},{5,4},{6,5},{7,6},{9,8},{10,9},{11,10},{12... | collective-permute-start | bytes 3145736 | tf_op jit(solution)/shard_map/ppermute | solution.py:14
  19.5 26.5 %collective-permute-start.2 = (bf16[2,16,16,256]{3,2,1,0:T(8,128)(2,1)}, bf16[2,16,16,256]{3,2,1,0:T(8,128)(2,1)S(1)}, u32[]{:S(2)}, u32[]{:S(2)}) collective-permute-start(bf16[2,16,16,256]{3,2,1,0:T(8,128)(2,1)} %slice.379), channel_id=1, source_target_pairs={{1,0},{2,1},{3,2},{4,3},{5,4},{6,5},{7,6},{9,8},{10,9},{11,10},{12... | collective-permute-start | bytes 786440 | tf_op jit(solution)/shard_map/ppermute | solution.py:14
  24.0 91.9 %copy-start.2 = (bf16[8,16,16,256]{3,2,1,0:T(8,128)(2,1)}, bf16[8,16,16,256]{3,2,1,0:T(8,128)(2,1)S(1)}, u32[]{:S(2)}) copy-start(bf16[8,16,16,256]{3,2,1,0:T(8,128)(2,1)S(1)} %gather_fusion) | copy-start | bytes 3145732
  53.3 2.5 copy-start.4
  53.3 2.5 copy-start.12
  56.3 1.2 copy-start.45
  57.5 1.2 copy-start.43
  59.3 1.2 copy-start.40
  60.6 1.2 copy-start.39
  61.8 1.2 copy-start.38
  63.0 1.2 copy-start.37
  64.2 1.2 copy-start.36
  65.5 1.2 copy-start.34
  67.9 1.2 copy-start.30
  69.6 1.2 copy-start.28
  70.8 1.2 copy-start.26
  72.1 1.2 copy-start.24
  73.3 1.2 copy-start.22
  74.5 1.2 copy-start.20
  75.7 1.2 copy-start.18
  77.0 1.2 copy-start.16
  80.6 1.2 copy-start.14
  83.6 32.3 %copy-start.50 = (f32[256]{0:T(256)S(1)}, f32[256]{0:T(256)}, u32[]{:S(2)}) copy-start(f32[256]{0:T(256)} %param.13) | copy-start | bytes 3076
  83.6 32.3 %copy-start.52 = (f32[256]{0:T(256)S(1)}, f32[256]{0:T(256)}, u32[]{:S(2)}) copy-start(f32[256]{0:T(256)} %param.14) | copy-start | bytes 3076
  120.7 6.6 %collective-permute-start.1 = (bf16[2,16,16,256]{3,2,1,0:T(8,128)(2,1)S(1)}, bf16[2,16,16,256]{3,2,1,0:T(8,128)(2,1)S(1)}, u32[]{:S(2)}, u32[]{:S(2)}) collective-permute-start(bf16[2,16,16,256]{3,2,1,0:T(8,128)(2,1)S(1)} %slice.374), channel_id=1, source_target_pairs={{0,1},{1,2},{2,3},{3,4},{4,5},{5,6},{6,7},{8,9},{9,10},{10,11},{11... | collective-permute-start | bytes 786440 | tf_op jit(solution)/shard_map/ppermute | solution.py:14
  127.3 15.5 %copy-start.48 = (bf16[2,16,16,256]{3,2,1,0:T(8,128)(2,1)}, bf16[2,16,16,256]{3,2,1,0:T(8,128)(2,1)S(1)}, u32[]{:S(2)}) copy-start(bf16[2,16,16,256]{3,2,1,0:T(8,128)(2,1)S(1)} %collective-permute-done.1) | copy-start | bytes 786436
  159.5 110.1 %copy-start.3 = (bf16[8,16,16,256]{3,2,1,0:T(8,128)(2,1)S(1)}, bf16[8,16,16,256]{3,2,1,0:T(8,128)(2,1)}, u32[]{:S(2)}) copy-start(bf16[8,16,16,256]{3,2,1,0:T(8,128)(2,1)} %copy-done.2) | copy-start | bytes 3145732
  159.5 356.1 %all-reduce.9.cloned.1.call-start = ((), (), s32[]{:S(2)}) async-start(), calls=%async_computation.1 | async-start | bytes 14155776 | tf_op jit(solution)/shard_map/psum | solution.py:139
  269.6 4.0 copy-start.49
  285.8 1.5 copy-start.47
  287.3 1.4 copy-start.46
  290.1 1.5 copy-start.44
  291.6 1.4 copy-start.42
  293.0 1.4 copy-start.41
  333.3 2.4 copy-start.5
  333.3 2.6 copy-start.35
  337.2 1.2 copy-start.31
  343.3 1.3 copy-start.23
  348.3 1.2 copy-start.15
  349.5 1.2 copy-start.10
  351.2 1.2 copy-start.9
  354.9 1.2 copy-start.13
  515.6 6.8 %copy-start.1 = (bf16[1,8,16,16,256]{4,3,2,1,0:T(8,128)(2,1)S(1)}, bf16[1,8,16,16,256]{4,3,2,1,0:T(8,128)(2,1)}, u32[]{:S(2)}) copy-start(bf16[1,8,16,16,256]{4,3,2,1,0:T(8,128)(2,1)} %param.9) | copy-start | bytes 3145732
  (11 other events, 13.5 us)
Sparse Core Ops, SparseCore 0:
  159.6 173.6 all-reduce.6
  335.8 179.6 all-reduce.8
